TPU v7x, 256 devices: a whole 4x4x8 slice. The times are simulated.
256 devices in a mesh: mem: 16 (over z, x_lo), lon: 16 (over x_hi, y, core).
Axes of the slice: x: 4 (x_hi: 2, x_lo: 2; x = x_hi * 2 + x_lo), y: 4, z: 8, core: 2. Of those that a mesh axis runs over, the one named last changes fastest.
Arguments:
- state: bfloat16 [256, 65536], P('mem', 'lon'), may hold values from -6 to 6
- hx: bfloat16 [512, 256, 128], P('lon'), may hold values from -6 to 6
- obs_value: float32 [512, 128], P('lon'), may hold values from -10 to 10
- obs_rinv: float32 [512, 128], P('lon'), may hold values from 0.3 to 3
- obs_count: int32 [512], P('lon'), may hold values from 1 to 128
- loc_pattern: int32 [512, 8], P('lon'), may hold values from 0 to 95, as said below
Outputs:
- analysis: bfloat16 [256, 65536], P('mem', 'lon')
Inputs may be any that keep to these rules, and one draw needn't show every extreme that they name: obs_count[n] is how many of block n's first observations are valid; the rest are ignored. Each row of loc_pattern holds 8 different window positions out of 96: the previous region's blocks, the patch's own region's blocks, the next region's blocks, around the closed longitude loop.
All inputs are finite; a program needn't handle non-finite values.
Results may differ from a plain program's by a relative error of at most 0.0065.
Values may be sent and summed in bfloat16 or wider, within the bound.
A program may use at most 64 MiB of HBM per device.

v0:
```python
import jax
import jax.numpy as jnp
from jax import lax
from jax.sharding import PartitionSpec as P

PAT_DEV = 2
USE = 8
ITERS = 6


def extended(value, sides, width):
    for axis, dim in sides:
        count, length = (lax.axis_size(axis), value.shape[dim])
        up = [(i, (i + 1) % count) for i in range(count)]
        down = [(j, i) for i, j in up]
        last = lax.slice_in_dim(value, length - width, length, axis=dim)
        first = lax.slice_in_dim(value, 0, width, axis=dim)
        before = lax.ppermute(last, axis, up)
        after = lax.ppermute(first, axis, down)
        value = jnp.concatenate([before, value, after], axis=dim)
    return value


def body(state, hx, obs_value, obs_rinv, obs_count, loc_pattern):
    high = lax.Precision.HIGHEST
    blocks = hx.shape[0]
    members = hx.shape[1]
    width_obs = hx.shape[2]
    mem_total = lax.axis_size("mem")
    mem_here = lax.axis_index("mem")
    region_patches = mem_total * PAT_DEV
    obs_mean = jnp.sum(hx, axis=1, dtype=jnp.float32) / members
    obs_pert = (hx.astype(jnp.float32) - obs_mean[:, None, :]).astype(jnp.bfloat16)
    valid = lax.broadcasted_iota(jnp.int32, (blocks, width_obs), 1) < obs_count[:, None]
    weight = jnp.where(valid, obs_rinv, jnp.float32(0.0))
    stats = jnp.stack([weight, weight * (obs_value - obs_mean)], axis=1).astype(jnp.bfloat16)
    picks = lax.dynamic_slice_in_dim(loc_pattern, mem_here * PAT_DEV, PAT_DEV, 0)
    ranks = (mem_here * PAT_DEV + jnp.arange(PAT_DEV, dtype=jnp.int32)).astype(jnp.float32)
    offset = (
        (picks.astype(jnp.float32) + 0.5) / blocks - 1.0 - (ranks[:, None] + 0.5) / region_patches
    )
    taper = jnp.exp(-0.5 * offset * offset)
    eye = jnp.eye(members, dtype=jnp.float32)
    system = jnp.broadcast_to((members - 1.0) * eye, (PAT_DEV, members, members))
    forcing = jnp.zeros((PAT_DEV, members), jnp.float32)
    window_pert, window_stats = (
        extended(obs_pert, (("lon", 0),), blocks),
        extended(stats, (("lon", 0),), blocks),
    )
    for slot in range(USE):
        chosen = picks[:, slot]
        picked_pert = window_pert[chosen]
        picked_stats = window_stats[chosen]
        scaled = (
            picked_stats[:, 0, None, :].astype(jnp.float32) * picked_pert.astype(jnp.float32)
        ).astype(jnp.bfloat16)
        gram = jnp.einsum("pkb,plb->pkl", picked_pert, scaled, preferred_element_type=jnp.float32)
        vec = jnp.einsum(
            "pkb,pb->pk", picked_pert, picked_stats[:, 1], preferred_element_type=jnp.float32
        )
        system = system + taper[:, slot, None, None] * gram
        forcing = forcing + taper[:, slot, None] * vec
    scale = jnp.sqrt(jnp.sum(system * system, axis=(1, 2)))
    iterate = system / scale[:, None, None]
    root = jnp.broadcast_to(eye, (PAT_DEV, members, members))
    for step in range(ITERS):
        factor = 1.5 * eye - 0.5 * jnp.einsum("pij,pjk->pik", root, iterate, precision=high)
        iterate = jnp.einsum("pij,pjk->pik", iterate, factor, precision=high)
        root = jnp.einsum("pij,pjk->pik", factor, root, precision=high)
    root = root / jnp.sqrt(scale)[:, None, None]
    inner = jnp.einsum("pij,pj->pi", root, forcing, precision=high)
    mean_weight = jnp.einsum("pij,pj->pi", root, inner, precision=high)
    transform = jnp.sqrt(jnp.float32(members - 1.0)) * root + mean_weight[:, :, None]
    local_members = state.shape[0]
    grid = state.reshape(local_members, region_patches, -1)
    gathered = lax.all_to_all(grid, "mem", split_axis=1, concat_axis=0, tiled=True)
    state_mean = jnp.sum(gathered, axis=0, dtype=jnp.float32) / members
    deviation = gathered.astype(jnp.float32) - state_mean[None]
    updated = state_mean[None] + jnp.einsum("pkl,kpt->lpt", transform, deviation, precision=high)
    result = lax.all_to_all(
        updated.astype(jnp.bfloat16), "mem", split_axis=0, concat_axis=1, tiled=True
    )
    return result.reshape(local_members, -1)


def solution(mesh):
    in_specs = (
        P("mem", "lon"),
        P("lon", None, None),
        P("lon", None),
        P("lon", None),
        P("lon"),
        P("lon", None),
    )
    out_specs = P("mem", "lon")
    return jax.shard_map(body, mesh=mesh, in_specs=in_specs, out_specs=out_specs, check_vma=False)
```

profile of v0, /device:TPU:2, one launch (start us, length us, event | category | flops | bytes accessed | tf_op | source)
XLA Modules:
  0.0 112.1 jit_solution(15731651959545263145)
XLA Ops:
  0.0 2.0 %convert_reduce_fusion = f32[32,128]{1,0:T(8,128)S(1)} fusion(bf16[32,256,128]{2,1,0:T(8,128)(2,1)} %param.7), kind=kLoop, calls=%fused_computation.18 | loop fusion | flops 2093056 | bytes 2113536 | tf_op jit(solution)/shard_map/reduce_sum | solution.py:32
  2.0 0.8 fusion.38
  2.8 0.8 fusion.39
  3.8 5.3 %collective-permute-start.3 = (bf16[32,2,128]{2,1,0:T(2,128)(2,1)S(1)}, bf16[32,2,128]{2,1,0:T(2,128)(2,1)S(1)}, u32[]{:S(2)}, u32[]{:S(2)}) collective-permute-start(bf16[32,2,128]{2,1,0:T(2,128)(2,1)S(1)} %pad_maximum_fusion.2), channel_id=1, source_target_pairs={{1,0},{2,1},{3,2},{4,3},{5,4},{6,5},{7,6},{8,7},{9,8},{10,9},{11,1... | collective-permute-start | bytes 49160 | tf_op jit(solution)/shard_map/ppermute | solution.py:19
  9.1 2.2 %fusion = bf16[32,256,128]{2,1,0:T(8,128)(2,1)S(1)} fusion(bf16[32,256,128]{2,1,0:T(8,128)(2,1)} %param.7, f32[32,128]{1,0:T(8,128)S(1)} %get-tuple-element.8), kind=kLoop, calls=%fused_computation.19 | loop fusion | flops 3145728 | bytes 4210688 | tf_op jit(solution)/shard_map/convert_element_type | solution.py:33
  11.4 5.3 %collective-permute-start.1 = (bf16[32,256,128]{2,1,0:T(8,128)(2,1)S(1)}, bf16[32,256,128]{2,1,0:T(8,128)(2,1)}, u32[]{:S(2)}, u32[]{:S(2)}) collective-permute-start(bf16[32,256,128]{2,1,0:T(8,128)(2,1)S(1)} %fusion), channel_id=1, source_target_pairs={{1,0},{2,1},{3,2},{4,3},{5,4},{6,5},{7,6},{8,7},{9,8},{10,9},{11,1... | collective-permute-start | bytes 6291464 | tf_op jit(solution)/shard_map/ppermute | solution.py:19
  16.7 0.7 copy_bitcast_fusion
  17.4 9.9 %all-to-all-start = ((bf16[16,32,128]{2,0,1:T(8,128)(2,1)}), bf16[16,32,128]{2,0,1:T(8,128)(2,1)S(1)}, u32[]{:S(2)}, u32[]{:S(2)}) async-start(bf16[16,32,128]{2,0,1:T(8,128)(2,1)} %copy_bitcast_fusion), calls=%async_computation | async-start | bytes 262144 | tf_op jit(solution)/shard_map/all_to_all | solution.py:76
  32.4 12.0 %all-to-all-done = bf16[16,32,128]{2,0,1:T(8,128)(2,1)S(1)} async-done(((bf16[16,32,128]{2,0,1:T(8,128)(2,1)}), bf16[16,32,128]{2,0,1:T(8,128)(2,1)S(1)}, u32[]{:S(2)}, u32[]{:S(2)}) %all-to-all-start) | async-done | bytes 131104 | tf_op jit(solution)/shard_map/all_to_all | solution.py:76
  44.5 0.7 bitcast_subtract_fusion
  45.3 5.5 %pad_maximum_fusion = bf16[96,256,128]{2,1,0:T(8,128)(2,1)} fusion(bf16[32,256,128]{2,1,0:T(8,128)(2,1)} %collective-permute-done.1, bf16[32,256,128]{2,1,0:T(8,128)(2,1)S(1)} %fusion, bf16[32,256,128]{2,1,0:T(8,128)(2,1)} %collective-permute-done), kind=kLoop, calls=%fused_computation.16 | loop fusion | flops 6291456 | bytes 12582912 | tf_op jit(solution)/shard_map/concatenate | solution.py:20
  50.8 3.4 %gather_fusion.12 = bf16[2,256,128]{2,1,0:T(8,128)(2,1)S(1)} fusion(bf16[96,256,128]{2,1,0:T(8,128)(2,1)} %pad_maximum_fusion, s32[1024]{0:T(1024)S(1)} %get-tuple-element.30), kind=kCustom, calls=%fused_computation.12 | custom fusion | bytes 262152 | tf_op jit(solution)/shard_map/gather | solution.py:52
  54.2 3.4 %gather_fusion.10 = bf16[2,256,128]{2,1,0:T(8,128)(2,1)S(1)} fusion(bf16[96,256,128]{2,1,0:T(8,128)(2,1)} %pad_maximum_fusion, s32[1024]{0:T(1024)S(1)} %get-tuple-element.31), kind=kCustom, calls=%fused_computation.10 | custom fusion | bytes 262152 | tf_op jit(solution)/shard_map/gather | solution.py:52
  57.5 3.4 %gather_fusion.8 = bf16[2,256,128]{2,1,0:T(8,128)(2,1)S(1)} fusion(bf16[96,256,128]{2,1,0:T(8,128)(2,1)} %pad_maximum_fusion, s32[1024]{0:T(1024)S(1)} %get-tuple-element.32), kind=kCustom, calls=%fused_computation.8 | custom fusion | bytes 262152 | tf_op jit(solution)/shard_map/gather | solution.py:52
  60.9 3.4 %gather_fusion.6 = bf16[2,256,128]{2,1,0:T(8,128)(2,1)S(1)} fusion(bf16[96,256,128]{2,1,0:T(8,128)(2,1)} %pad_maximum_fusion, s32[1024]{0:T(1024)S(1)} %get-tuple-element.33), kind=kCustom, calls=%fused_computation.6 | custom fusion | bytes 262152 | tf_op jit(solution)/shard_map/gather | solution.py:52
  64.3 3.4 %gather_fusion.4 = bf16[2,256,128]{2,1,0:T(8,128)(2,1)S(1)} fusion(bf16[96,256,128]{2,1,0:T(8,128)(2,1)} %pad_maximum_fusion, s32[1024]{0:T(1024)S(1)} %get-tuple-element.34), kind=kCustom, calls=%fused_computation.4 | custom fusion | bytes 262152 | tf_op jit(solution)/shard_map/gather | solution.py:52
  67.6 3.4 %gather_fusion.2 = bf16[2,256,128]{2,1,0:T(8,128)(2,1)S(1)} fusion(bf16[96,256,128]{2,1,0:T(8,128)(2,1)} %pad_maximum_fusion, s32[1024]{0:T(1024)S(1)} %get-tuple-element.35), kind=kCustom, calls=%fused_computation.2 | custom fusion | bytes 262152 | tf_op jit(solution)/shard_map/gather | solution.py:52
  71.0 3.4 %gather_fusion = bf16[2,256,128]{2,1,0:T(8,128)(2,1)S(1)} fusion(bf16[96,256,128]{2,1,0:T(8,128)(2,1)} %pad_maximum_fusion, s32[1024]{0:T(1024)S(1)} %get-tuple-element.36), kind=kCustom, calls=%fused_computation | custom fusion | bytes 262152 | tf_op jit(solution)/shard_map/gather | solution.py:52
  74.3 3.4 %gather_fusion.14 = bf16[2,256,128]{2,1,0:T(8,128)(2,1)S(1)} fusion(bf16[96,256,128]{2,1,0:T(8,128)(2,1)} %pad_maximum_fusion, s32[1024]{0:T(1024)S(1)} %get-tuple-element.29), kind=kCustom, calls=%fused_computation.14 | custom fusion | bytes 262152 | tf_op jit(solution)/shard_map/gather | solution.py:52
  81.0 0.7 fusion.6
  81.8 0.7 fusion.35
  83.1 0.7 fusion.5
  85.1 0.7 fusion.4
  85.7 0.7 fusion.73
  87.1 0.7 fusion.3
  87.7 0.7 fusion.75
  89.1 0.7 fusion.2
  91.1 0.9 fusion.1
  91.9 0.7 convolution_divide_fusion
  93.8 0.7 fusion.16
  94.7 16.5 %all_to_all.24 = bf16[256,2,128]{2,1,0:T(2,128)(2,1)S(1)} all-to-all(bf16[256,2,128]{2,1,0:T(2,128)(2,1)S(1)} %copy.46), channel_id=1, replica_groups=mesh['mem'=16,'lon'=16] {'mem'}, dimensions={0} | all-to-all | bytes 262144 | tf_op jit(solution)/shard_map/all_to_all | solution.py:80
  111.3 0.7 reshape.53
  (80 shorter events, 14.5 us)
Async XLA Ops:
  0.0 16.7 %copy-start = (bf16[16,4096]{1,0:T(8,128)(2,1)S(1)}, bf16[16,4096]{1,0:T(8,128)(2,1)}, u32[]{:S(2)}) copy-start(bf16[16,4096]{1,0:T(8,128)(2,1)} %param.6) | copy-start | bytes 393220
  0.0 27.5 %copy-start.2 = (s32[32,8]{0,1:T(8,128)S(1)}, s32[32,8]{0,1:T(8,128)}, u32[]{:S(2)}) copy-start(s32[32,8]{0,1:T(8,128)} %param.11) | copy-start | bytes 3076
  3.7 24.0 %collective-permute-start.2 = (bf16[32,2,128]{2,1,0:T(2,128)(2,1)S(1)}, bf16[32,2,128]{2,1,0:T(2,128)(2,1)S(1)}, u32[]{:S(2)}, u32[]{:S(2)}) collective-permute-start(bf16[32,2,128]{2,1,0:T(2,128)(2,1)S(1)} %pad_maximum_fusion.2), channel_id=1, source_target_pairs={{0,1},{1,2},{2,3},{3,4},{4,5},{5,6},{6,7},{7,8},{8,9},{9,10},{10,1... | collective-permute-start | bytes 49160 | tf_op jit(solution)/shard_map/ppermute | solution.py:18
  3.8 23.9 %collective-permute-start.3 = (bf16[32,2,128]{2,1,0:T(2,128)(2,1)S(1)}, bf16[32,2,128]{2,1,0:T(2,128)(2,1)S(1)}, u32[]{:S(2)}, u32[]{:S(2)}) collective-permute-start(bf16[32,2,128]{2,1,0:T(2,128)(2,1)S(1)} %pad_maximum_fusion.2), channel_id=1, source_target_pairs={{1,0},{2,1},{3,2},{4,3},{5,4},{6,5},{7,6},{8,7},{9,8},{10,9},{11,1... | collective-permute-start | bytes 49160 | tf_op jit(solution)/shard_map/ppermute | solution.py:19
  11.3 34.0 %collective-permute-start = (bf16[32,256,128]{2,1,0:T(8,128)(2,1)S(1)}, bf16[32,256,128]{2,1,0:T(8,128)(2,1)}, u32[]{:S(2)}, u32[]{:S(2)}) collective-permute-start(bf16[32,256,128]{2,1,0:T(8,128)(2,1)S(1)} %fusion), channel_id=1, source_target_pairs={{0,1},{1,2},{2,3},{3,4},{4,5},{5,6},{6,7},{7,8},{8,9},{9,10},{10,1... | collective-permute-start | bytes 6291464 | tf_op jit(solution)/shard_map/ppermute | solution.py:18
  11.4 33.9 %collective-permute-start.1 = (bf16[32,256,128]{2,1,0:T(8,128)(2,1)S(1)}, bf16[32,256,128]{2,1,0:T(8,128)(2,1)}, u32[]{:S(2)}, u32[]{:S(2)}) collective-permute-start(bf16[32,256,128]{2,1,0:T(8,128)(2,1)S(1)} %fusion), channel_id=1, source_target_pairs={{1,0},{2,1},{3,2},{4,3},{5,4},{6,5},{7,6},{8,7},{9,8},{10,9},{11,1... | collective-permute-start | bytes 6291464 | tf_op jit(solution)/shard_map/ppermute | solution.py:19
  17.4 27.0 %all-to-all-start = ((bf16[16,32,128]{2,0,1:T(8,128)(2,1)}), bf16[16,32,128]{2,0,1:T(8,128)(2,1)S(1)}, u32[]{:S(2)}, u32[]{:S(2)}) async-start(bf16[16,32,128]{2,0,1:T(8,128)(2,1)} %copy_bitcast_fusion), calls=%async_computation | async-start | bytes 262144 | tf_op jit(solution)/shard_map/all_to_all | solution.py:76
  87.7 6.1 %copy-start.1 = (f32[256,2,128]{2,0,1:T(8,128)S(1)}, f32[256,2,128]{2,0,1:T(8,128)}, u32[]{:S(2)}) copy-start(f32[256,2,128]{2,0,1:T(8,128)} %bitcast_subtract_fusion) | copy-start | bytes 786436
where the time goes:
time: 114 us; the launch traced here: 112 us
  local copies, waits for them, and re-layouts  33.2 us (29%)
  starting transfers between devices  20.8 us (18%)
  matrix products  16.5 us (14%)
  blocking collectives  16.5 us (14%)
  other arithmetic  12.5 us (11%)
  waiting for transfers between devices  12 us (11%)
    gather x8, local copies, waits for them, and re-layouts, body(): picked_pert = window_pert[chosen]  26.9 us
    all_to_all x1, blocking collectives, body(): lax.all_to_all(updated.astype(jnp.bfloat16), 'mem', split_axis=0, concat_...  16.5 us
    all_to_all x1, waiting for transfers between devices, body(): lax.all_to_all(grid, 'mem', split_axis=1, concat_axis=0, tiled=True)  12 us
    ppermute x2, starting transfers between devices, extended(): after = lax.ppermute(first, axis, down)  10.7 us
    all_to_all x1, starting transfers between devices, body(): lax.all_to_all(grid, 'mem', split_axis=1, concat_axis=0, tiled=True)  9.94 us
    concatenate x2, other arithmetic, extended(): value = jnp.concatenate([before, value, after], axis=dim)  5.6 us
    gather x8, local copies, waits for them, and re-layouts, body(): picked_stats = window_stats[chosen]  4.57 us
    dot_general x6, matrix products, body(): jnp.einsum('pij,pjk->pik', root, iterate, precision=high)  4.22 us
  transfers between devices with their start and end apart: 5, of which 1 were waited for; matrix products, arithmetic and copies ran while one was open for 8% of the time, Pallas kernels for 0%

commit v1 on v0

v1 whole, which is shorter than its diff:
```python
import functools

import jax
import jax.numpy as jnp
from jax import lax
from jax.experimental import pallas as pl
from jax.experimental.pallas import tpu as pltpu
from jax.sharding import PartitionSpec as P

MESH = pl.DeviceIdType.MESH
F32, BF16 = jnp.float32, jnp.bfloat16
USE = 8
PAT = 2
EXTRA = 16
CHUNKS = 4
E_STEPS = 3


def dot(a, b):
    return lax.dot_general(a, b, (((1,), (0,)), ((), ())), preferred_element_type=F32)


def dot_nt(a, b):
    return lax.dot_general(a, b, (((1,), (1,)), ((), ())), preferred_element_type=F32)


def kernel(
    n_mem, n_lon,
    state_ref, hx_ref, value_ref, rinv_ref, count_ref, loc_ref,
    out_ref,
    pert, weight, innov, lhs, rhs, own, send, recv, gathered, rows, answer, loc_far,
    hx_sem, here_sem, loc_send, loc_recv, part_send, part_recv, in_send, in_recv, ans_send, ans_recv,
):
    mem, lon = lax.axis_index("mem"), lax.axis_index("lon")
    blocks, members, width = hx_ref.shape
    local = state_ref.shape[0]
    cols = state_ref.shape[1] // n_mem
    pts = cols // PAT
    ranks = n_mem * PAT

    odd = lon % 2
    sign = 2 * odd - 1
    wrap = (lon + odd) % 8 == 0
    crossed = mem + 1 - 2 * (mem % 2)
    partners = (
        ((lon + sign + n_lon) % n_lon, jnp.where(wrap, crossed, mem), sign),
        ((lon - sign + n_lon) % n_lon, mem, -sign),
    )

    per = blocks // CHUNKS
    fetches = []
    for c in range(CHUNKS):
        part = pl.ds(c * per, per)
        fetch = pltpu.make_async_copy(hx_ref.at[part], pert.at[part], hx_sem.at[c])
        fetch.start()
        fetches.append(fetch)
    mine_rows = pl.ds(pl.multiple_of(mem * local, local), local)
    mine_cols = pl.ds(pl.multiple_of(mem * cols, cols), cols)
    keep = pltpu.make_async_copy(state_ref.at[:, mine_cols], gathered.at[mine_rows, :], here_sem.at[0])
    keep.start()

    barrier = pltpu.get_barrier_semaphore()
    for p_lon, p_mem, _ in partners:
        pl.semaphore_signal(barrier, inc=1, device_id=(p_mem, p_lon), device_id_type=MESH)
    peers = [(mem + d) % n_mem for d in range(1, n_mem)]
    for peer in peers:
        pl.semaphore_signal(barrier, inc=1, device_id=(peer, lon), device_id_type=MESH)

    lane = lax.broadcasted_iota(jnp.int32, (1, width), 1)

    def prepare(b):
        x = pert[b].astype(F32)
        mean = jnp.sum(x, axis=0, keepdims=True) * (1.0 / members)
        pert[b] = (x - mean).astype(BF16)
        w = jnp.where(lane < count_ref[b], rinv_ref[pl.ds(b, 1), :], 0.0)
        weight[pl.ds(b, 1), :] = w.astype(BF16).astype(F32)
        innov[pl.ds(b, 1), :] = (w * (value_ref[pl.ds(b, 1), :] - mean)).astype(BF16).astype(F32)

    for c in range(CHUNKS):
        fetches[c].wait()

        @pl.loop(0, per // 4)
        def _(g):
            for k in range(4):
                prepare(c * per + g * 4 + k)

    pl.semaphore_wait(barrier, n_mem + 1)

    loc_moves = []
    for q, (p_lon, p_mem, _) in enumerate(partners):
        move = pltpu.make_async_remote_copy(
            src_ref=loc_ref, dst_ref=loc_far.at[q],
            send_sem=loc_send.at[q], recv_sem=loc_recv.at[q],
            device_id=(p_mem, p_lon), device_id_type=MESH,
        )
        move.start()
        loc_moves.append(move)
    state_moves = []
    for d, peer in enumerate(peers):
        theirs = pl.ds(pl.multiple_of(peer * cols, cols), cols)
        move = pltpu.make_async_remote_copy(
            src_ref=state_ref.at[:, theirs], dst_ref=gathered.at[mine_rows, :],
            send_sem=in_send.at[d], recv_sem=in_recv.at[d],
            device_id=(peer, lon), device_id_type=MESH,
        )
        move.start()
        state_moves.append(move)

    sub = lax.broadcasted_iota(jnp.int32, (EXTRA, width), 0)

    def partial(picks, base, rank):
        for s in range(USE):
            u = picks(s)
            rel = u - base
            inside = jnp.logical_and(rel >= 0, rel < blocks)
            b = jnp.clip(rel, 0, blocks - 1)
            uf = jnp.full((1, width), u, jnp.int32).astype(F32)
            rf = jnp.full((1, width), rank, jnp.int32).astype(F32)
            t = (uf + 0.5) / blocks - 1.0 - (rf + 0.5) / ranks
            taper = jnp.exp(-0.5 * t * t) * jnp.full((1, width), inside.astype(jnp.int32), jnp.int32).astype(F32)
            block = pert[b]
            w = jnp.broadcast_to(weight[pl.ds(b, 1), :] * taper, (EXTRA, width)).astype(BF16)
            scaled = (block.reshape(members // EXTRA, EXTRA, width) * w[None]).reshape(members, width)
            v = jnp.broadcast_to(innov[pl.ds(b, 1), :] * taper, (EXTRA, width))
            high = v.astype(BF16).astype(F32)
            tail = jnp.where(sub == 0, high, jnp.where(sub == 1, v - high, 0.0)).astype(BF16)
            at = pl.ds(s * width, width)
            lhs[pl.ds(0, members), at] = scaled
            lhs[pl.ds(members, EXTRA), at] = tail
            rhs[:, at] = block
        return dot_nt(lhs[...], rhs[...])

    for j in range(PAT):
        rank = mem * PAT + j
        own[j] = partial(lambda s: loc_ref[rank, s], blocks, rank)

    row_id = lax.broadcasted_iota(jnp.int32, (EXTRA, members), 0)
    part_moves = []
    for q, (p_lon, p_mem, s_q) in enumerate(partners):
        loc_moves[q].wait_recv()
        for j in range(PAT):
            rank = p_mem * PAT + j
            got = partial(lambda s: loc_far[q, rank, s], blocks - blocks * s_q, rank)
            send[q, j, pl.ds(0, members), :] = got[:members].astype(BF16)
            force = got[members : members + 1] + got[members + 1 : members + 2]
            high = force.astype(BF16).astype(F32)
            both = jnp.where(row_id == 0, high, jnp.where(row_id == 1, force - high, 0.0))
            send[q, j, pl.ds(members, EXTRA), :] = both.astype(BF16)
            move = pltpu.make_async_remote_copy(
                src_ref=send.at[q, j], dst_ref=recv.at[q, j],
                send_sem=part_send.at[q, j], recv_sem=part_recv.at[q, j],
                device_id=(p_mem, p_lon), device_id_type=MESH,
            )
            move.start()
            part_moves.append(move)

    keep.wait()
    for move in state_moves:
        move.wait_recv()
    g = gathered[...].astype(F32)
    state_mean = jnp.sum(g, axis=0, keepdims=True) * (1.0 / members)
    rows[...] = (g - state_mean).T

    diag = lax.broadcasted_iota(jnp.int32, (members, members), 0) == lax.broadcasted_iota(
        jnp.int32, (members, members), 1
    )
    for move in part_moves:
        move.wait_recv()

    mats, carried, scales = [], [], []
    for j in range(PAT):
        a = own[j, pl.ds(0, members), :]
        force = own[j, pl.ds(members, 1), :] + own[j, pl.ds(members + 1, 1), :]
        for q in range(2):
            a = a + recv[q, j, pl.ds(0, members), :].astype(F32)
            f = recv[q, j, pl.ds(members, EXTRA), :].astype(F32)
            force = force + f[0:1] + f[1:2]
        a = a + jnp.where(diag, members - 1.0, 0.0)
        norm2 = jnp.sum(jnp.sum(a * a, axis=0, keepdims=True), axis=1, keepdims=True)
        inv = lax.rsqrt(norm2)
        mats.append(a * inv)
        scales.append(jnp.sqrt(inv))
        pad = jnp.where(row_id[:8] == 0, jnp.broadcast_to(force, (8, members)), 0.0)
        carried.append(jnp.concatenate([rows[pl.ds(j * pts, pts), :], pad], axis=0))

    for step in range(6):
        for j in range(PAT):
            e = mats[j]
            eb = e.astype(BF16)
            moved = dot(carried[j].astype(BF16), eb)
            if step < E_STEPS:
                carried[j] = 1.5 * carried[j] - 0.5 * moved
            else:
                carried[j] = carried[j] + 0.5 * moved
            if step < 5:
                square = dot(eb, eb)
                cube = dot(square.astype(BF16), eb)
                if step < E_STEPS:
                    e = 2.25 * e - 1.5 * square + 0.25 * cube
                    if step == E_STEPS - 1:
                        e = jnp.where(diag, 1.0, 0.0) - e
                else:
                    e = 0.75 * square + 0.25 * cube
                mats[j] = e

    for j in range(PAT):
        x = carried[j] * scales[j]
        d, u = x[:pts], x[pts : pts + 1]
        shift = jnp.sum(d * u, axis=1, keepdims=True)
        y = (jnp.sqrt(jnp.float32(members - 1.0)) * d + shift).T
        at = pl.ds(j * pts, pts)
        answer[:, at] = (y + state_mean[:, j * pts : (j + 1) * pts]).astype(BF16)

    stay = pltpu.make_async_copy(answer.at[mine_rows, :], out_ref.at[:, mine_cols], here_sem.at[1])
    stay.start()
    ans_moves = []
    for d, peer in enumerate(peers):
        theirs = pl.ds(pl.multiple_of(peer * local, local), local)
        move = pltpu.make_async_remote_copy(
            src_ref=answer.at[theirs, :], dst_ref=out_ref.at[:, mine_cols],
            send_sem=ans_send.at[d], recv_sem=ans_recv.at[d],
            device_id=(peer, lon), device_id_type=MESH,
        )
        move.start()
        ans_moves.append(move)
    for move in loc_moves + state_moves + part_moves:
        move.wait_send()
    stay.wait()
    for move in ans_moves:
        move.wait()


def solution(mesh):
    n_mem, n_lon = mesh.shape["mem"], mesh.shape["lon"]

    def body(state, hx, obs_value, obs_rinv, obs_count, loc_pattern):
        blocks, members, width = hx.shape
        local, points = state.shape
        cols = points // n_mem
        peers = n_mem - 1
        high = members + EXTRA
        dma = pltpu.SemaphoreType.DMA
        any_, vmem, smem = (pl.BlockSpec(memory_space=s) for s in (pl.ANY, pltpu.VMEM, pltpu.SMEM))
        return pl.pallas_call(
            functools.partial(kernel, n_mem, n_lon),
            out_shape=jax.ShapeDtypeStruct((local, points), BF16),
            in_specs=[any_, any_, vmem, vmem, smem, smem],
            out_specs=OUT_SPEC,
            scratch_shapes=[
                pltpu.VMEM((blocks, members, width), BF16),
                pltpu.VMEM((blocks, width), F32),
                pltpu.VMEM((blocks, width), F32),
                pltpu.VMEM((high, USE * width), BF16),
                pltpu.VMEM((members, USE * width), BF16),
                pltpu.VMEM((PAT, high, members), F32),
                pltpu.VMEM((2, PAT, high, members), BF16),
                pltpu.VMEM((2, PAT, high, members), BF16),
                pltpu.VMEM((members, cols), BF16),
                pltpu.VMEM((cols, members), F32),
                pltpu.VMEM((members, cols), BF16),
                pltpu.SMEM((2,) + loc_pattern.shape, jnp.int32),
                dma((CHUNKS,)),
                dma((2,)),
                dma((2,)),
                dma((2,)),
                dma((2, PAT)),
                dma((2, PAT)),
                dma((peers,)),
                dma((peers,)),
                dma((peers,)),
                dma((peers,)),
            ],
            compiler_params=pltpu.CompilerParams(collective_id=0, has_side_effects=True, vmem_limit_bytes=48 << 20),
        )(state, hx, obs_value, obs_rinv, obs_count, loc_pattern)

    in_specs = (
        P("mem", "lon"),
        P("lon", None, None),
        P("lon", None),
        P("lon", None),
        P("lon"),
        P("lon", None),
    )
    return jax.shard_map(body, mesh=mesh, in_specs=in_specs, out_specs=P("mem", "lon"), check_vma=False)


OUT_SPEC = pl.BlockSpec(memory_space=pltpu.VMEM)
```

time: 114 us -> 36.4 us (0.32); the launches traced: 112 us -> 36.1 us
  Pallas kernels: 0 us -> 30.1 us
  local copies, waits for them, and re-layouts: 33.2 us -> 6 us
  starting transfers between devices: 20.8 us -> 0 us
  matrix products: 16.5 us -> 0 us
  blocking collectives: 16.5 us -> 0 us
  other arithmetic: 12.5 us -> 0 us
  waiting for transfers between devices: 12 us -> 0 us
    gather x16 -> x0, local copies, waits for them, and re-layouts: 31.4 us -> none  [the longest x8 26.9 us: body(): picked_pert = window_pert[chosen]]
    pallas_call x0 -> x1, Pallas kernels: none -> 30.1 us  [body(): pl.pallas_call(functools.partial(kernel, n_mem, n_lon), out_shape=jax.Sha...]
    all_to_all x1 -> x0, blocking collectives: 16.5 us -> none  [body(): lax.all_to_all(updated.astype(jnp.bfloat16), 'mem', split_axis=0, concat_...]
    dot_general x36 -> x0, matrix products: 16.5 us -> none  [the longest x6 4.22 us: body(): jnp.einsum('pij,pjk->pik', root, iterate, precision=high)]
    all_to_all x1 -> x0, waiting for transfers between devices: 12 us -> none  [body(): lax.all_to_all(grid, 'mem', split_axis=1, concat_axis=0, tiled=True)]
    ppermute x4 -> x0, starting transfers between devices: 10.9 us -> none  [the longest x2 10.7 us: extended(): after = lax.ppermute(first, axis, down)]
    all_to_all x1 -> x0, starting transfers between devices: 9.94 us -> none  [body(): lax.all_to_all(grid, 'mem', split_axis=1, concat_axis=0, tiled=True)]
    unnamed x6 -> x12, local copies, waits for them, and re-layouts: 0.02 us -> 6 us
  transfers between devices with their start and end apart: 5 -> 0, of which waited for: 1 -> 0; matrix products, arithmetic and copies ran while one was open for 8% -> 0% of each run, Pallas kernels for 0% -> 0%
where the time goes in v1:
time: 36.4 us; the launch traced here: 36.1 us
  Pallas kernels  30.1 us (83%)
  local copies, waits for them, and re-layouts  6 us (16%)
    pallas_call x1, Pallas kernels, body(): pl.pallas_call(functools.partial(kernel, n_mem, n_lon), out_shape=jax.Sha...  30.1 us
    unnamed x12, local copies, waits for them, and re-layouts  6 us

profile of v1, /device:TPU:2, one launch (start us, length us, event | category | flops | bytes accessed | tf_op | source)
XLA Modules:
  0.0 36.1 jit_solution(3178569558624787878)
XLA Ops:
  0.0 0.8 %copy.7.loc_ref = s32[32,8]{1,0:T(8,128)S(1)} copy(s32[32,8]{0,1:T(8,128)} %param.11) | data formatting | bytes 2048 | tf_op args[5]
  0.8 0.0 copy-start
  0.8 1.6 %copy-done = bf16[32,256,128]{2,1,0:T(8,128)(2,1)S(1)} copy-done((bf16[32,256,128]{2,1,0:T(8,128)(2,1)S(1)}, bf16[32,256,128]{2,1,0:T(8,128)(2,1)}, u32[]{:S(2)}) %copy-start) | copy-done | bytes 2097176
  2.4 0.0 copy-start.1
  2.4 0.9 %copy-done.1 = bf16[16,4096]{1,0:T(8,128)(2,1)S(1)} copy-done((bf16[16,4096]{1,0:T(8,128)(2,1)S(1)}, bf16[16,4096]{1,0:T(8,128)(2,1)}, u32[]{:S(2)}) %copy-start.1) | copy-done | bytes 131096
  3.3 0.0 copy-start.2
  3.3 0.7 %copy-done.2 = f32[32,128]{1,0:T(8,128)S(1)} copy-done((f32[32,128]{1,0:T(8,128)S(1)}, f32[32,128]{1,0:T(8,128)}, u32[]{:S(2)}) %copy-start.2) | copy-done | bytes 16408
  4.0 0.0 copy-start.3
  4.0 0.7 %copy-done.3 = f32[32,128]{1,0:T(8,128)S(1)} copy-done((f32[32,128]{1,0:T(8,128)S(1)}, f32[32,128]{1,0:T(8,128)}, u32[]{:S(2)}) %copy-start.3) | copy-done | bytes 16408
  4.7 0.0 copy-start.4
  4.7 0.7 %copy-done.4 = s32[32]{0:T(128)S(1)} copy-done((s32[32]{0:T(128)S(1)}, s32[32]{0:T(128)}, u32[]{:S(2)}) %copy-start.4) | copy-done | bytes 152
  5.3 30.1 %shard_map.64 = bf16[16,4096]{1,0:T(8,128)(2,1)S(1)} custom-call(bf16[16,4096]{1,0:T(8,128)(2,1)S(1)} %copy-done.1, bf16[32,256,128]{2,1,0:T(8,128)(2,1)S(1)} %copy-done, f32[32,128]{1,0:T(8,128)S(1)} %copy-done.2, f32[32,128]{1,0:T(8,128)S(1)} %copy-done.3, s32[32]{0:T(128)S(1)} %copy-done.4, s32[32,8]{1,0:T(8,128)S(1)} %copy.7.loc_ref), custom_call_target="tpu_custom_call" | custom-call | tf_op jit(solution)/shard_map/pallas_call | solution.py:244
  35.4 0.7 %copy.9 = bf16[16,4096]{1,0:T(8,128)(2,1)} copy(bf16[16,4096]{1,0:T(8,128)(2,1)S(1)} %shard_map.64) | data formatting | bytes 262144
Async XLA Ops:
  0.8 1.6 %copy-start = (bf16[32,256,128]{2,1,0:T(8,128)(2,1)S(1)}, bf16[32,256,128]{2,1,0:T(8,128)(2,1)}, u32[]{:S(2)}) copy-start(bf16[32,256,128]{2,1,0:T(8,128)(2,1)} %hx_ref.1) | copy-start | bytes 6291460
  2.4 0.9 %copy-start.1 = (bf16[16,4096]{1,0:T(8,128)(2,1)S(1)}, bf16[16,4096]{1,0:T(8,128)(2,1)}, u32[]{:S(2)}) copy-start(bf16[16,4096]{1,0:T(8,128)(2,1)} %state_ref.1) | copy-start | bytes 393220
  3.3 0.7 %copy-start.2 = (f32[32,128]{1,0:T(8,128)S(1)}, f32[32,128]{1,0:T(8,128)}, u32[]{:S(2)}) copy-start(f32[32,128]{1,0:T(8,128)} %value_ref.1) | copy-start | bytes 49156
  4.0 0.7 %copy-start.3 = (f32[32,128]{1,0:T(8,128)S(1)}, f32[32,128]{1,0:T(8,128)}, u32[]{:S(2)}) copy-start(f32[32,128]{1,0:T(8,128)} %rinv_ref.1) | copy-start | bytes 49156
  4.7 0.7 %copy-start.4 = (s32[32]{0:T(128)S(1)}, s32[32]{0:T(128)}, u32[]{:S(2)}) copy-start(s32[32]{0:T(128)} %count_ref.1) | copy-start | bytes 388

commit v2 on v1

v2 whole, which is shorter than its diff:
```python
import functools

import jax
import jax.numpy as jnp
from jax import lax
from jax.experimental import pallas as pl
from jax.experimental.pallas import tpu as pltpu
from jax.sharding import PartitionSpec as P

MESH = pl.DeviceIdType.MESH
F32, BF16 = jnp.float32, jnp.bfloat16
USE = 8
PAT = 2
TAIL = 16
CHUNKS = 4
ITERS = 6
E_STEPS = 3


def dot(a, b):
    return lax.dot_general(a, b, (((1,), (0,)), ((), ())), preferred_element_type=F32)


def dot_nt(a, b):
    return lax.dot_general(a, b, (((1,), (1,)), ((), ())), preferred_element_type=F32)


def halves(x):
    high = x.astype(BF16).astype(F32)
    return high, x - high


def kernel(
    n_mem, n_lon,
    state_ref, hx_ref, value_hbm, rinv_hbm, count_hbm, loc_hbm,
    out_ref,
    pert, value_ref, rinv_ref, count_ref, loc_ref, weight, innov, lhs, rhs, own, own_tail, send, recv, gathered, answer, loc_far,
    hx_sem, small_sem, here_sem, loc_send, loc_recv, part_send, part_recv, in_send, in_recv, ans_send, ans_recv,
    near_sem, far_sem, side_sem,
):
    mem, lon = lax.axis_index("mem"), lax.axis_index("lon")
    blocks, members, width = hx_ref.shape
    half = members // 2
    local = state_ref.shape[0]
    cols = state_ref.shape[1] // n_mem
    pts = cols // PAT
    ranks = n_mem * PAT
    n_z = n_mem // 2
    z, x = mem // 2, mem % 2

    odd = lon % 2
    sign = 2 * odd - 1
    wrap = (lon + odd) % 8 == 0
    crossed = mem + 1 - 2 * x
    partners = (
        ((lon + sign + n_lon) % n_lon, jnp.where(wrap, crossed, mem), sign),
        ((lon - sign + n_lon) % n_lon, mem, -sign),
    )

    def along(step):
        return ((z + step + n_z) % n_z) * 2 + x

    def signal(sem, to_mem, to_lon):
        pl.semaphore_signal(sem, inc=1, device_id=(to_mem, to_lon), device_id_type=MESH)

    barrier = pltpu.get_barrier_semaphore()
    for p_lon, p_mem, _ in partners:
        signal(barrier, p_mem, p_lon)
    for step in (1, -1):
        signal(barrier, along(step), lon)
    signal(barrier, crossed, lon)

    smalls = []
    for i, (src, dst) in enumerate(
        ((loc_hbm, loc_ref), (count_hbm, count_ref), (rinv_hbm, rinv_ref), (value_hbm, value_ref))
    ):
        move = pltpu.make_async_copy(src, dst, small_sem.at[i])
        move.start()
        smalls.append(move)
    per = blocks // CHUNKS
    fetches = []
    for c in range(CHUNKS):
        part = pl.ds(c * per, per)
        fetch = pltpu.make_async_copy(hx_ref.at[part], pert.at[part], hx_sem.at[c])
        fetch.start()
        fetches.append(fetch)
    mine_rows = pl.ds(pl.multiple_of(mem * local, local), local)
    mine_cols = pl.ds(pl.multiple_of(mem * cols, cols), cols)
    keep = pltpu.make_async_copy(state_ref.at[:, mine_cols], gathered.at[mine_rows, :], here_sem.at[0])
    keep.start()
    for move in smalls:
        move.wait()

    lane = lax.broadcasted_iota(jnp.int32, (1, width), 1)

    def prepare(b):
        v = pert[b].astype(F32)
        mean = jnp.sum(v, axis=0, keepdims=True) * (1.0 / members)
        pert[b] = (v - mean).astype(BF16)
        w = jnp.where(lane < count_ref[b], rinv_ref[pl.ds(b, 1), :], 0.0)
        weight[pl.ds(b, 1), :] = w.astype(BF16).astype(F32)
        innov[pl.ds(b, 1), :] = (w * (value_ref[pl.ds(b, 1), :] - mean)).astype(BF16).astype(F32)

    def prepare_chunk(c):
        fetches[c].wait()

        @pl.loop(0, per // 4)
        def _(g):
            for k in range(4):
                prepare(c * per + g * 4 + k)

    for c in range(CHUNKS // 2):
        prepare_chunk(c)

    pl.semaphore_wait(barrier, 5)
    loc_moves = []
    for q, (p_lon, p_mem, _) in enumerate(partners):
        move = pltpu.make_async_remote_copy(
            src_ref=loc_ref, dst_ref=loc_far.at[q],
            send_sem=loc_send.at[q], recv_sem=loc_recv.at[q],
            device_id=(p_mem, p_lon), device_id_type=MESH,
        )
        move.start()
        loc_moves.append(move)
    for step in (1, -1):
        signal(near_sem, along(step), lon)

    for c in range(CHUNKS // 2, CHUNKS):
        prepare_chunk(c)

    sub = lax.broadcasted_iota(jnp.int32, (TAIL, width), 0)
    row_i = lax.broadcasted_iota(jnp.int32, (half, half), 0)
    col_i = lax.broadcasted_iota(jnp.int32, (half, half), 1)

    def partial(picks, base, rank):
        for s in range(USE):
            u = picks(s)
            rel = u - base
            inside = jnp.logical_and(rel >= 0, rel < blocks)
            b = jnp.clip(rel, 0, blocks - 1)
            uf = jnp.full((1, width), u, jnp.int32).astype(F32)
            rf = jnp.full((1, width), rank, jnp.int32).astype(F32)
            t = (uf + 0.5) / blocks - 1.0 - (rf + 0.5) / ranks
            taper = jnp.exp(-0.5 * t * t) * jnp.full((1, width), inside.astype(jnp.int32), jnp.int32).astype(F32)
            block = pert[b]
            scaled = (block.astype(F32) * (weight[pl.ds(b, 1), :] * taper)).astype(BF16)
            high, low = halves(jnp.broadcast_to(innov[pl.ds(b, 1), :] * taper, (TAIL, width)))
            tail = jnp.where(sub == 0, high, jnp.where(sub == 1, low, 0.0)).astype(BF16)
            at = pl.ds(s * width, width)
            lhs[pl.ds(0, members), at] = scaled
            lhs[pl.ds(members, TAIL), at] = tail
            rhs[:, at] = block
        got = dot_nt(lhs[...], rhs[...])
        top, low = got[:half, :half], got[half:members, half:]
        packed = jnp.concatenate([jnp.where(row_i <= col_i, top, low), got[:half, half:]], axis=1)
        diag = jnp.concatenate(
            [jnp.sum(jnp.where(row_i == col_i, m, 0.0), axis=0, keepdims=True) for m in (top, low)], axis=1
        )
        return packed, got[members : members + 1] + got[members + 1 : members + 2], diag

    for j in range(PAT):
        rank = mem * PAT + j
        packed, force, diag = partial(lambda s: loc_ref[s, rank], blocks, rank)
        own[j] = packed
        own_tail[j, pl.ds(0, 1), :] = force
        own_tail[j, pl.ds(1, 1), :] = diag

    pl.semaphore_wait(near_sem, 2)
    for step in (2, -2):
        signal(far_sem, along(step), lon)

    row_id = lax.broadcasted_iota(jnp.int32, (TAIL, members), 0)
    part_moves = []
    for q, (p_lon, p_mem, s_q) in enumerate(partners):
        loc_moves[q].wait_recv()
        for j in range(PAT):
            rank = p_mem * PAT + j
            packed, force, diag = partial(lambda s: loc_far[q, s, rank], blocks - blocks * s_q, rank)
            send[q, j, pl.ds(0, half), :] = packed.astype(BF16)
            tail = jnp.zeros((TAIL, members), F32)
            for i, line in enumerate(halves(force) + halves(diag)):
                tail = jnp.where(row_id == i, line, tail)
            send[q, j, pl.ds(half, TAIL), :] = tail.astype(BF16)
            move = pltpu.make_async_remote_copy(
                src_ref=send.at[q, j], dst_ref=recv.at[q, j],
                send_sem=part_send.at[q, j], recv_sem=part_recv.at[q, j],
                device_id=(p_mem, p_lon), device_id_type=MESH,
            )
            move.start()
            part_moves.append(move)
        if q == 0:
            pl.semaphore_wait(far_sem, 2)
            signal(side_sem, crossed, lon)

    pl.semaphore_wait(side_sem, 1)
    order = []
    for step in (4, 3, -3, 2, -2, 1, -1, 0):
        column = (z + step + n_z) % n_z
        order.append(column * 2 + 1 - x)
        if step:
            order.append(column * 2 + x)
    state_moves = []
    for d, peer in enumerate(order):
        theirs = pl.ds(pl.multiple_of(peer * cols, cols), cols)
        move = pltpu.make_async_remote_copy(
            src_ref=state_ref.at[:, theirs], dst_ref=gathered.at[mine_rows, :],
            send_sem=in_send.at[d], recv_sem=in_recv.at[d],
            device_id=(peer, lon), device_id_type=MESH,
        )
        move.start()
        state_moves.append(move)

    eye = jnp.where(
        lax.broadcasted_iota(jnp.int32, (members, members), 0)
        == lax.broadcasted_iota(jnp.int32, (members, members), 1),
        1.0,
        0.0,
    )
    for move in part_moves:
        move.wait_recv()

    mats, roots, forces, scales = [], [], [], []
    for j in range(PAT):
        packed = own[j]
        force, diag = own_tail[j, pl.ds(0, 1), :], own_tail[j, pl.ds(1, 1), :]
        for q in range(2):
            packed = packed + recv[q, j, pl.ds(0, half), :].astype(F32)
            lines = recv[q, j, pl.ds(half, TAIL), :].astype(F32)
            force = force + lines[0:1] + lines[1:2]
            diag = diag + lines[2:3] + lines[3:4]
        diag = diag + (members - 1.0)
        mixed, cross = packed[:, :half], packed[:, half:]
        turned = mixed.T
        top = jnp.where(row_i == col_i, diag[:, :half], jnp.where(row_i < col_i, mixed, turned))
        low = jnp.where(row_i == col_i, diag[:, half:], jnp.where(row_i > col_i, mixed, turned))
        a = jnp.concatenate(
            [jnp.concatenate([top, cross], axis=1), jnp.concatenate([cross.T, low], axis=1)], axis=0
        )
        norm2 = jnp.sum(jnp.sum(a * a, axis=0, keepdims=True), axis=1, keepdims=True)
        inv = lax.rsqrt(norm2)
        mats.append(a * inv)
        scales.append(jnp.sqrt(inv))
        roots.append(None)
        forces.append(jnp.where(row_id == 0, jnp.broadcast_to(force, (TAIL, members)), 0.0))

    for step in range(ITERS):
        for j in range(PAT):
            e = mats[j]
            eb = e.astype(BF16)
            early = step < E_STEPS
            lead, gain = (1.5, -0.5) if early else (1.0, 0.5)
            forces[j] = lead * forces[j] + gain * dot(forces[j].astype(BF16), eb)
            if step == 0:
                roots[j] = lead * eye + gain * e
            else:
                roots[j] = lead * roots[j] + gain * dot(roots[j].astype(BF16), eb)
            if step < ITERS - 1:
                square = dot(eb, eb)
                cube = dot(square.astype(BF16), eb)
                if early:
                    e = 2.25 * e - 1.5 * square + 0.25 * cube
                    if step == E_STEPS - 1:
                        e = eye - e
                else:
                    e = 0.75 * square + 0.25 * cube
                mats[j] = e

    weights, rest = [], []
    for j in range(PAT):
        root = roots[j] * scales[j]
        mean_weight = dot((forces[j] * scales[j]).astype(BF16), root.astype(BF16))[0:1]
        w = jnp.sqrt(jnp.float32(members - 1.0)) * root + mean_weight
        high = w.astype(BF16)
        low = (w - high.astype(F32)).astype(BF16)
        weights.append((high, low))
        rest.append(1.0 - jnp.sum(w, axis=1, keepdims=True))

    keep.wait()
    for move in state_moves:
        move.wait_recv()
    ones = jnp.ones((TAIL, members), BF16)
    for j in range(PAT):
        at = pl.ds(j * pts, pts)
        points = gathered[:, at]
        high, low = weights[j]
        mean = dot(ones, points)[0:1] * (1.0 / members)
        answer[:, at] = (dot(high, points) + dot(low, points) + rest[j] * mean).astype(BF16)

    ans_moves = []
    for d, peer in enumerate(order):
        theirs = pl.ds(pl.multiple_of(peer * local, local), local)
        move = pltpu.make_async_remote_copy(
            src_ref=answer.at[theirs, :], dst_ref=out_ref.at[:, mine_cols],
            send_sem=ans_send.at[d], recv_sem=ans_recv.at[d],
            device_id=(peer, lon), device_id_type=MESH,
        )
        move.start()
        ans_moves.append(move)
    stay = pltpu.make_async_copy(answer.at[mine_rows, :], out_ref.at[:, mine_cols], here_sem.at[1])
    stay.start()
    for move in loc_moves + state_moves + part_moves:
        move.wait_send()
    stay.wait()
    for move in ans_moves:
        move.wait()


def solution(mesh):
    n_mem, n_lon = mesh.shape["mem"], mesh.shape["lon"]

    def body(state, hx, obs_value, obs_rinv, obs_count, loc_pattern):
        blocks, members, width = hx.shape
        local, points = state.shape
        cols = points // n_mem
        peers = n_mem - 1
        packed = members // 2 + TAIL
        dma, regular = pltpu.SemaphoreType.DMA, pltpu.SemaphoreType.REGULAR
        picks = loc_pattern.T
        args = (state, hx, obs_value, obs_rinv, obs_count, picks)
        return pl.pallas_call(
            functools.partial(kernel, n_mem, n_lon),
            out_shape=jax.ShapeDtypeStruct((local, points), BF16),
            in_specs=[pl.BlockSpec(memory_space=pl.ANY)] * len(args),
            out_specs=pl.BlockSpec(memory_space=pltpu.VMEM),
            scratch_shapes=[
                pltpu.VMEM((blocks, members, width), BF16),
                pltpu.VMEM((blocks, width), F32),
                pltpu.VMEM((blocks, width), F32),
                pltpu.SMEM((blocks,), jnp.int32),
                pltpu.SMEM(picks.shape, jnp.int32),
                pltpu.VMEM((blocks, width), F32),
                pltpu.VMEM((blocks, width), F32),
                pltpu.VMEM((members + TAIL, USE * width), BF16),
                pltpu.VMEM((members, USE * width), BF16),
                pltpu.VMEM((PAT, members // 2, members), F32),
                pltpu.VMEM((PAT, 8, members), F32),
                pltpu.VMEM((2, PAT, packed, members), BF16),
                pltpu.VMEM((2, PAT, packed, members), BF16),
                pltpu.VMEM((members, cols), BF16),
                pltpu.VMEM((members, cols), BF16),
                pltpu.SMEM((2,) + picks.shape, jnp.int32),
                dma((CHUNKS,)),
                dma((4,)),
                dma((2,)),
                dma((2,)),
                dma((2,)),
                dma((2, PAT)),
                dma((2, PAT)),
                dma((peers,)),
                dma((peers,)),
                dma((peers,)),
                dma((peers,)),
                regular,
                regular,
                regular,
            ],
            compiler_params=pltpu.CompilerParams(
                collective_id=0, has_side_effects=True, vmem_limit_bytes=LIMIT
            ),
        )(*args)

    in_specs = (
        P("mem", "lon"),
        P("lon", None, None),
        P("lon", None),
        P("lon", None),
        P("lon"),
        P("lon", None),
    )
    return jax.shard_map(body, mesh=mesh, in_specs=in_specs, out_specs=P("mem", "lon"), check_vma=False)


LIMIT = 63 << 20
```

time: 36.4 us -> 29.5 us (0.81)
  local copies, waits for them, and re-layouts: 6 us -> 1.57 us
  Pallas kernels: 30.1 us -> 27.8 us
    unnamed x12 -> x1, local copies, waits for them, and re-layouts: 6 us -> 1.57 us
    pallas_call x1, Pallas kernels: 30.1 us -> 27.8 us  [body(): pl.pallas_call(functools.partial(kernel, n_mem, n_lon), out_shape=jax.Sha...]
where the time goes in v2:
time: 29.5 us; the launch traced here: 29.4 us
  Pallas kernels  27.8 us (94%)
  local copies, waits for them, and re-layouts  1.57 us (5%)
    pallas_call x1, Pallas kernels, body(): pl.pallas_call(functools.partial(kernel, n_mem, n_lon), out_shape=jax.Sha...  27.8 us
    unnamed x1, local copies, waits for them, and re-layouts  1.57 us

profile of v2, /device:TPU:2, one launch (start us, length us, event | category | flops | bytes accessed | tf_op | source)
XLA Modules:
  0.0 29.4 jit_solution(14125799707559482412)
XLA Ops:
  0.0 27.8 %shard_map.64 = bf16[16,4096]{1,0:T(8,128)(2,1)} custom-call(bf16[16,4096]{1,0:T(8,128)(2,1)} %state_ref.1, bf16[32,256,128]{2,1,0:T(8,128)(2,1)} %hx_ref.1, f32[32,128]{1,0:T(8,128)} %value_hbm.1, f32[32,128]{1,0:T(8,128)} %rinv_hbm.1, s32[32]{0:T(128)} %count_hbm.1, s32[8,32]{1,0:T(8,128)} %bitcast.1), custom_call_target="tpu_custom_call" | custom-call | tf_op jit(solution)/shard_map/pallas_call | solution.py:320
  27.8 1.6 %copy.8 = bf16[16,4096]{1,0:T(8,128)(2,1)} copy(bf16[16,4096]{1,0:T(8,128)(2,1)} %shard_map.64) | data formatting | bytes 262144

commit v3 on v2

--- a/solution.py
+++ b/solution.py
@@ -14,7 +14,7 @@
 TAIL = 16
 CHUNKS = 4
 ITERS = 6
-E_STEPS = 3
+E_STEPS = 4
 
 
 def dot(a, b):
@@ -169,8 +169,17 @@
     for step in (2, -2):
         signal(far_sem, along(step), lon)
 
+    pl.semaphore_wait(far_sem, 2)
+    signal(side_sem, crossed, lon)
+
+    order = []
+    for step in (4, 3, -3, 2, -2, 1, -1, 0):
+        column = (z + step + n_z) % n_z
+        order.append(column * 2 + 1 - x)
+        if step:
+            order.append(column * 2 + x)
     row_id = lax.broadcasted_iota(jnp.int32, (TAIL, members), 0)
-    part_moves = []
+    part_moves, state_moves = [], []
     for q, (p_lon, p_mem, s_q) in enumerate(partners):
         loc_moves[q].wait_recv()
         for j in range(PAT):
@@ -189,26 +198,16 @@
             move.start()
             part_moves.append(move)
         if q == 0:
-            pl.semaphore_wait(far_sem, 2)
-            signal(side_sem, crossed, lon)
-
-    pl.semaphore_wait(side_sem, 1)
-    order = []
-    for step in (4, 3, -3, 2, -2, 1, -1, 0):
-        column = (z + step + n_z) % n_z
-        order.append(column * 2 + 1 - x)
-        if step:
-            order.append(column * 2 + x)
-    state_moves = []
-    for d, peer in enumerate(order):
-        theirs = pl.ds(pl.multiple_of(peer * cols, cols), cols)
-        move = pltpu.make_async_remote_copy(
-            src_ref=state_ref.at[:, theirs], dst_ref=gathered.at[mine_rows, :],
-            send_sem=in_send.at[d], recv_sem=in_recv.at[d],
-            device_id=(peer, lon), device_id_type=MESH,
-        )
-        move.start()
-        state_moves.append(move)
+            pl.semaphore_wait(side_sem, 1)
+            for d, peer in enumerate(order):
+                theirs = pl.ds(pl.multiple_of(peer * cols, cols), cols)
+                move = pltpu.make_async_remote_copy(
+                    src_ref=state_ref.at[:, theirs], dst_ref=gathered.at[mine_rows, :],
+                    send_sem=in_send.at[d], recv_sem=in_recv.at[d],
+                    device_id=(peer, lon), device_id_type=MESH,
+                )
+                move.start()
+                state_moves.append(move)
 
     eye = jnp.where(
         lax.broadcasted_iota(jnp.int32, (members, members), 0)
@@ -219,7 +218,7 @@
     for move in part_moves:
         move.wait_recv()
 
-    mats, roots, forces, scales = [], [], [], []
+    mats, raws, roots, forces, scales = [], [], [], [], []
     for j in range(PAT):
         packed = own[j]
         force, diag = own_tail[j, pl.ds(0, 1), :], own_tail[j, pl.ds(1, 1), :]
@@ -239,9 +238,17 @@
         norm2 = jnp.sum(jnp.sum(a * a, axis=0, keepdims=True), axis=1, keepdims=True)
         inv = lax.rsqrt(norm2)
         mats.append(a * inv)
+        raws.append((a.astype(BF16), inv))
         scales.append(jnp.sqrt(inv))
         roots.append(None)
-        forces.append(jnp.where(row_id == 0, jnp.broadcast_to(force, (TAIL, members)), 0.0))
+        forces.append(force)
+
+    def stacked(line):
+        high, low = halves(line)
+        return jnp.where(row_id == 0, high, jnp.where(row_id == 1, low, 0.0)).astype(BF16)
+
+    def sum_rows(m):
+        return m[0:1] + m[1:2]
 
     for step in range(ITERS):
         for j in range(PAT):
@@ -249,13 +256,17 @@
             eb = e.astype(BF16)
             early = step < E_STEPS
             lead, gain = (1.5, -0.5) if early else (1.0, 0.5)
-            forces[j] = lead * forces[j] + gain * dot(forces[j].astype(BF16), eb)
+            forces[j] = lead * forces[j] + gain * sum_rows(dot(stacked(forces[j]), eb))
             if step == 0:
                 roots[j] = lead * eye + gain * e
             else:
                 roots[j] = lead * roots[j] + gain * dot(roots[j].astype(BF16), eb)
             if step < ITERS - 1:
-                square = dot(eb, eb)
+                if step == 0:
+                    raw, inv = raws[j]
+                    square = dot(raw, raw) * (inv * inv)
+                else:
+                    square = dot(eb, eb)
                 cube = dot(square.astype(BF16), eb)
                 if early:
                     e = 2.25 * e - 1.5 * square + 0.25 * cube
@@ -268,7 +279,9 @@
     weights, rest = [], []
     for j in range(PAT):
         root = roots[j] * scales[j]
-        mean_weight = dot((forces[j] * scales[j]).astype(BF16), root.astype(BF16))[0:1]
+        high, low = halves(root)
+        u = stacked(forces[j] * scales[j])
+        mean_weight = sum_rows(dot(u, high.astype(BF16)) + dot(u, low.astype(BF16)))
         w = jnp.sqrt(jnp.float32(members - 1.0)) * root + mean_weight
         high = w.astype(BF16)
         low = (w - high.astype(F32)).astype(BF16)
@@ -319,7 +332,7 @@
         args = (state, hx, obs_value, obs_rinv, obs_count, picks)
         return pl.pallas_call(
             functools.partial(kernel, n_mem, n_lon),
-            out_shape=jax.ShapeDtypeStruct((local, points), BF16),
+            out_shape=pltpu.VMEM((local, points), BF16),
             in_specs=[pl.BlockSpec(memory_space=pl.ANY)] * len(args),
             out_specs=pl.BlockSpec(memory_space=pltpu.VMEM),
             scratch_shapes=[

time: 29.5 us -> 28 us (0.949)
  local copies, waits for them, and re-layouts: 1.57 us -> 0.66 us
  Pallas kernels: 27.8 us -> 27.2 us
    unnamed x1, local copies, waits for them, and re-layouts: 1.57 us -> 0.66 us
    pallas_call x1, Pallas kernels: 27.8 us -> 27.2 us  [body(): pl.pallas_call(functools.partial(kernel, n_mem, n_lon), out_shape=pltpu.V...]
where the time goes in v3:
time: 28 us; the launch traced here: 27.9 us
  Pallas kernels  27.2 us (97%)
  local copies, waits for them, and re-layouts  0.66 us (2%)
    pallas_call x1, Pallas kernels, body(): pl.pallas_call(functools.partial(kernel, n_mem, n_lon), out_shape=pltpu.V...  27.2 us
    unnamed x1, local copies, waits for them, and re-layouts  0.66 us

profile of v3, /device:TPU:2, one launch (start us, length us, event | category | flops | bytes accessed | tf_op | source)
XLA Modules:
  0.0 27.9 jit_solution(10864549895463992679)
XLA Ops:
  0.0 27.2 %shard_map.64 = bf16[16,4096]{1,0:T(8,128)(2,1)S(1)} custom-call(bf16[16,4096]{1,0:T(8,128)(2,1)} %state_ref.1, bf16[32,256,128]{2,1,0:T(8,128)(2,1)} %hx_ref.1, f32[32,128]{1,0:T(8,128)} %value_hbm.1, f32[32,128]{1,0:T(8,128)} %rinv_hbm.1, s32[32]{0:T(128)} %count_hbm.1, s32[8,32]{1,0:T(8,128)} %bitcast.1), custom_call_target="tpu_custom_call" | custom-call | tf_op jit(solution)/shard_map/pallas_call | solution.py:333
  27.2 0.7 %copy.8 = bf16[16,4096]{1,0:T(8,128)(2,1)} copy(bf16[16,4096]{1,0:T(8,128)(2,1)S(1)} %shard_map.64) | data formatting | bytes 262144

commit v4 on v3

--- a/solution.py
+++ b/solution.py
@@ -15,6 +15,7 @@
 CHUNKS = 4
 ITERS = 6
 E_STEPS = 4
+AHEAD = 2
 
 
 def dot(a, b):
@@ -34,9 +35,8 @@
     n_mem, n_lon,
     state_ref, hx_ref, value_hbm, rinv_hbm, count_hbm, loc_hbm,
     out_ref,
-    pert, value_ref, rinv_ref, count_ref, loc_ref, weight, innov, lhs, rhs, own, own_tail, send, recv, gathered, answer, loc_far,
+    pert, value_ref, rinv_ref, count_ref, loc_ref, weight, innov, own, own_tail, send, recv, gathered, answer, loc_far,
     hx_sem, small_sem, here_sem, loc_send, loc_recv, part_send, part_recv, in_send, in_recv, ans_send, ans_recv,
-    near_sem, far_sem, side_sem,
 ):
     mem, lon = lax.axis_index("mem"), lax.axis_index("lon")
     blocks, members, width = hx_ref.shape
@@ -66,9 +66,14 @@
     barrier = pltpu.get_barrier_semaphore()
     for p_lon, p_mem, _ in partners:
         signal(barrier, p_mem, p_lon)
-    for step in (1, -1):
-        signal(barrier, along(step), lon)
-    signal(barrier, crossed, lon)
+    order = []
+    for step in (4, 3, -3, 2, -2, 1, -1, 0):
+        column = (z + step + n_z) % n_z
+        order.append(column * 2 + 1 - x)
+        if step:
+            order.append(column * 2 + x)
+    for peer in order:
+        signal(barrier, peer, lon)
 
     smalls = []
     for i, (src, dst) in enumerate(
@@ -112,7 +117,7 @@
     for c in range(CHUNKS // 2):
         prepare_chunk(c)
 
-    pl.semaphore_wait(barrier, 5)
+    pl.semaphore_wait(barrier, len(partners) + len(order))
     loc_moves = []
     for q, (p_lon, p_mem, _) in enumerate(partners):
         move = pltpu.make_async_remote_copy(
@@ -122,8 +127,16 @@
         )
         move.start()
         loc_moves.append(move)
-    for step in (1, -1):
-        signal(near_sem, along(step), lon)
+    state_moves = []
+    for d, peer in enumerate(order):
+        theirs = pl.ds(pl.multiple_of(peer * cols, cols), cols)
+        move = pltpu.make_async_remote_copy(
+            src_ref=state_ref.at[:, theirs], dst_ref=gathered.at[mine_rows, :],
+            send_sem=in_send.at[d], recv_sem=in_recv.at[d],
+            device_id=(peer, lon), device_id_type=MESH,
+        )
+        move.start()
+        state_moves.append(move)
 
     for c in range(CHUNKS // 2, CHUNKS):
         prepare_chunk(c)
@@ -133,6 +146,7 @@
     col_i = lax.broadcasted_iota(jnp.int32, (half, half), 1)
 
     def partial(picks, base, rank):
+        left, right = [], []
         for s in range(USE):
             u = picks(s)
             rel = u - base
@@ -146,11 +160,9 @@
             scaled = (block.astype(F32) * (weight[pl.ds(b, 1), :] * taper)).astype(BF16)
             high, low = halves(jnp.broadcast_to(innov[pl.ds(b, 1), :] * taper, (TAIL, width)))
             tail = jnp.where(sub == 0, high, jnp.where(sub == 1, low, 0.0)).astype(BF16)
-            at = pl.ds(s * width, width)
-            lhs[pl.ds(0, members), at] = scaled
-            lhs[pl.ds(members, TAIL), at] = tail
-            rhs[:, at] = block
-        got = dot_nt(lhs[...], rhs[...])
+            left.append(jnp.concatenate([scaled, tail], axis=0))
+            right.append(block)
+        got = dot_nt(jnp.concatenate(left, axis=1), jnp.concatenate(right, axis=1))
         top, low = got[:half, :half], got[half:members, half:]
         packed = jnp.concatenate([jnp.where(row_i <= col_i, top, low), got[:half, half:]], axis=1)
         diag = jnp.concatenate(
@@ -165,21 +177,8 @@
         own_tail[j, pl.ds(0, 1), :] = force
         own_tail[j, pl.ds(1, 1), :] = diag
 
-    pl.semaphore_wait(near_sem, 2)
-    for step in (2, -2):
-        signal(far_sem, along(step), lon)
-
-    pl.semaphore_wait(far_sem, 2)
-    signal(side_sem, crossed, lon)
-
-    order = []
-    for step in (4, 3, -3, 2, -2, 1, -1, 0):
-        column = (z + step + n_z) % n_z
-        order.append(column * 2 + 1 - x)
-        if step:
-            order.append(column * 2 + x)
     row_id = lax.broadcasted_iota(jnp.int32, (TAIL, members), 0)
-    part_moves, state_moves = [], []
+    part_moves = []
     for q, (p_lon, p_mem, s_q) in enumerate(partners):
         loc_moves[q].wait_recv()
         for j in range(PAT):
@@ -197,17 +196,6 @@
             )
             move.start()
             part_moves.append(move)
-        if q == 0:
-            pl.semaphore_wait(side_sem, 1)
-            for d, peer in enumerate(order):
-                theirs = pl.ds(pl.multiple_of(peer * cols, cols), cols)
-                move = pltpu.make_async_remote_copy(
-                    src_ref=state_ref.at[:, theirs], dst_ref=gathered.at[mine_rows, :],
-                    send_sem=in_send.at[d], recv_sem=in_recv.at[d],
-                    device_id=(peer, lon), device_id_type=MESH,
-                )
-                move.start()
-                state_moves.append(move)
 
     eye = jnp.where(
         lax.broadcasted_iota(jnp.int32, (members, members), 0)
@@ -218,7 +206,7 @@
     for move in part_moves:
         move.wait_recv()
 
-    mats, raws, roots, forces, scales = [], [], [], [], []
+    mats, raws, forces, scales = [], [], [], []
     for j in range(PAT):
         packed = own[j]
         force, diag = own_tail[j, pl.ds(0, 1), :], own_tail[j, pl.ds(1, 1), :]
@@ -237,10 +225,10 @@
         )
         norm2 = jnp.sum(jnp.sum(a * a, axis=0, keepdims=True), axis=1, keepdims=True)
         inv = lax.rsqrt(norm2)
-        mats.append(a * inv)
-        raws.append((a.astype(BF16), inv))
-        scales.append(jnp.sqrt(inv))
-        roots.append(None)
+        third = inv * (1.0 / 3.0)
+        mats.append(a * third)
+        raws.append((a.astype(BF16), third))
+        scales.append(jnp.sqrt(inv) * 1.5**E_STEPS)
         forces.append(force)
 
     def stacked(line):
@@ -250,54 +238,65 @@
     def sum_rows(m):
         return m[0:1] + m[1:2]
 
-    for step in range(ITERS):
+    loads, units = [], []
+    for j in range(PAT):
+        loads.append([raws[j][0]])
+        units.append(raws[j][1])
+
+    def raise_step(j, step):
+        e, eb = mats[j], loads[j][step]
+        square = dot(eb, eb)
+        if step == 0:
+            square = square * (units[j] * units[j])
+        cube = dot(square.astype(BF16), eb)
+        if step == 0:
+            cube = cube * units[j]
+        if step < E_STEPS:
+            e = ((e - square) - square) + cube
+            mats[j] = 2.25 * e if step < E_STEPS - 1 else 0.5 * eye - 3.375 * e
+        else:
+            mats[j] = 1.5 * square + cube
+        loads[j].append(mats[j].astype(BF16))
+
+    for step in range(AHEAD):
         for j in range(PAT):
-            e = mats[j]
-            eb = e.astype(BF16)
-            early = step < E_STEPS
-            lead, gain = (1.5, -0.5) if early else (1.0, 0.5)
-            forces[j] = lead * forces[j] + gain * sum_rows(dot(stacked(forces[j]), eb))
-            if step == 0:
-                roots[j] = lead * eye + gain * e
-            else:
-                roots[j] = lead * roots[j] + gain * dot(roots[j].astype(BF16), eb)
-            if step < ITERS - 1:
-                if step == 0:
-                    raw, inv = raws[j]
-                    square = dot(raw, raw) * (inv * inv)
-                else:
-                    square = dot(eb, eb)
-                cube = dot(square.astype(BF16), eb)
-                if early:
-                    e = 2.25 * e - 1.5 * square + 0.25 * cube
-                    if step == E_STEPS - 1:
-                        e = eye - e
-                else:
-                    e = 0.75 * square + 0.25 * cube
-                mats[j] = e
-
-    weights, rest = [], []
-    for j in range(PAT):
-        root = roots[j] * scales[j]
-        high, low = halves(root)
-        u = stacked(forces[j] * scales[j])
-        mean_weight = sum_rows(dot(u, high.astype(BF16)) + dot(u, low.astype(BF16)))
-        w = jnp.sqrt(jnp.float32(members - 1.0)) * root + mean_weight
-        high = w.astype(BF16)
-        low = (w - high.astype(F32)).astype(BF16)
-        weights.append((high, low))
-        rest.append(1.0 - jnp.sum(w, axis=1, keepdims=True))
+            raise_step(j, step)
 
     keep.wait()
     for move in state_moves:
         move.wait_recv()
-    ones = jnp.ones((TAIL, members), BF16)
+    points = gathered[...].astype(F32)
+    state_mean = jnp.sum(points, axis=0, keepdims=True) * (1.0 / members)
+    turned = (points - state_mean).T
+    rows = [turned[j * pts : (j + 1) * pts] for j in range(PAT)]
+
+    def apply_step(j, step):
+        left = jnp.concatenate([rows[j].astype(BF16), stacked(forces[j])], axis=0)
+        moved = dot(left, loads[j][step])
+        if step == 0:
+            moved = moved * units[j]
+        force = sum_rows(moved[pts:])
+        if step < E_STEPS:
+            rows[j], forces[j] = rows[j] - moved[:pts], forces[j] - force
+        else:
+            rows[j], forces[j] = rows[j] + moved[:pts], forces[j] + force
+
+    done = 0
+    for step in range(AHEAD, ITERS):
+        for j in range(PAT):
+            if step < ITERS - 1:
+                raise_step(j, step)
+        upto = ITERS if step == ITERS - 1 else step + 1
+        for k in range(done, upto):
+            for j in range(PAT):
+                apply_step(j, k)
+        done = upto
+
     for j in range(PAT):
-        at = pl.ds(j * pts, pts)
-        points = gathered[:, at]
-        high, low = weights[j]
-        mean = dot(ones, points)[0:1] * (1.0 / members)
-        answer[:, at] = (dot(high, points) + dot(low, points) + rest[j] * mean).astype(BF16)
+        s = scales[j]
+        shift = jnp.sum(rows[j] * (forces[j] * (s * s)), axis=1, keepdims=True)
+        y = (rows[j] * (s * jnp.sqrt(jnp.float32(members - 1.0))) + shift).T
+        answer[:, pl.ds(j * pts, pts)] = (y + state_mean[:, j * pts : (j + 1) * pts]).astype(BF16)
 
     ans_moves = []
     for d, peer in enumerate(order):
@@ -327,7 +326,7 @@
         cols = points // n_mem
         peers = n_mem - 1
         packed = members // 2 + TAIL
-        dma, regular = pltpu.SemaphoreType.DMA, pltpu.SemaphoreType.REGULAR
+        dma = pltpu.SemaphoreType.DMA
         picks = loc_pattern.T
         args = (state, hx, obs_value, obs_rinv, obs_count, picks)
         return pl.pallas_call(
@@ -343,8 +342,6 @@
                 pltpu.SMEM(picks.shape, jnp.int32),
                 pltpu.VMEM((blocks, width), F32),
                 pltpu.VMEM((blocks, width), F32),
-                pltpu.VMEM((members + TAIL, USE * width), BF16),
-                pltpu.VMEM((members, USE * width), BF16),
                 pltpu.VMEM((PAT, members // 2, members), F32),
                 pltpu.VMEM((PAT, 8, members), F32),
                 pltpu.VMEM((2, PAT, packed, members), BF16),
@@ -363,9 +360,6 @@
                 dma((peers,)),
                 dma((peers,)),
                 dma((peers,)),
-                regular,
-                regular,
-                regular,
             ],
             compiler_params=pltpu.CompilerParams(
                 collective_id=0, has_side_effects=True, vmem_limit_bytes=LIMIT

time: 28 us -> 27.1 us (0.968)
  Pallas kernels: 27.2 us -> 26.3 us
    pallas_call x1, Pallas kernels: 27.2 us -> 26.3 us  [body(): pl.pallas_call(functools.partial(kernel, n_mem, n_lon), out_shape=pltpu.V...]
where the time goes in v4:
time: 27.1 us; the launch traced here: 27 us
  Pallas kernels  26.3 us (97%)
  local copies, waits for them, and re-layouts  0.66 us (2%)
    pallas_call x1, Pallas kernels, body(): pl.pallas_call(functools.partial(kernel, n_mem, n_lon), out_shape=pltpu.V...  26.3 us
    unnamed x1, local copies, waits for them, and re-layouts  0.66 us

profile of v4, /device:TPU:2, one launch (start us, length us, event | category | flops | bytes accessed | tf_op | source)
XLA Modules:
  0.0 27.0 jit_solution(15870369972171499543)
XLA Ops:
  0.0 26.3 %shard_map.64 = bf16[16,4096]{1,0:T(8,128)(2,1)S(1)} custom-call(bf16[16,4096]{1,0:T(8,128)(2,1)} %state_ref.1, bf16[32,256,128]{2,1,0:T(8,128)(2,1)} %hx_ref.1, f32[32,128]{1,0:T(8,128)} %value_hbm.1, f32[32,128]{1,0:T(8,128)} %rinv_hbm.1, s32[32]{0:T(128)} %count_hbm.1, s32[8,32]{1,0:T(8,128)} %bitcast.1), custom_call_target="tpu_custom_call" | custom-call | tf_op jit(solution)/shard_map/pallas_call | solution.py:332
  26.3 0.7 %copy.8 = bf16[16,4096]{1,0:T(8,128)(2,1)} copy(bf16[16,4096]{1,0:T(8,128)(2,1)S(1)} %shard_map.64) | data formatting | bytes 262144

commit v5 on v4

--- a/solution.py
+++ b/solution.py
@@ -15,7 +15,7 @@
 CHUNKS = 4
 ITERS = 6
 E_STEPS = 4
-AHEAD = 2
+AHEAD = 1
 
 
 def dot(a, b):
@@ -203,6 +203,14 @@
         1.0,
         0.0,
     )
+    keep.wait()
+    for move in state_moves:
+        move.wait_recv()
+    points = gathered[...].astype(F32)
+    state_mean = jnp.sum(points, axis=0, keepdims=True) * (1.0 / members)
+    across = (points - state_mean).T
+    rows = [across[j * pts : (j + 1) * pts] for j in range(PAT)]
+
     for move in part_moves:
         move.wait_recv()
 
@@ -258,18 +266,6 @@
             mats[j] = 1.5 * square + cube
         loads[j].append(mats[j].astype(BF16))
 
-    for step in range(AHEAD):
-        for j in range(PAT):
-            raise_step(j, step)
-
-    keep.wait()
-    for move in state_moves:
-        move.wait_recv()
-    points = gathered[...].astype(F32)
-    state_mean = jnp.sum(points, axis=0, keepdims=True) * (1.0 / members)
-    turned = (points - state_mean).T
-    rows = [turned[j * pts : (j + 1) * pts] for j in range(PAT)]
-
     def apply_step(j, step):
         left = jnp.concatenate([rows[j].astype(BF16), stacked(forces[j])], axis=0)
         moved = dot(left, loads[j][step])
@@ -281,16 +277,15 @@
         else:
             rows[j], forces[j] = rows[j] + moved[:pts], forces[j] + force
 
-    done = 0
-    for step in range(AHEAD, ITERS):
+    for step in range(ITERS - 1 + AHEAD):
         for j in range(PAT):
             if step < ITERS - 1:
                 raise_step(j, step)
-        upto = ITERS if step == ITERS - 1 else step + 1
-        for k in range(done, upto):
-            for j in range(PAT):
-                apply_step(j, k)
-        done = upto
+        for j in range(PAT):
+            if 0 <= step - AHEAD:
+                apply_step(j, step - AHEAD)
+    for j in range(PAT):
+        apply_step(j, ITERS - 1)
 
     for j in range(PAT):
         s = scales[j]

time: 27.1 us -> 27 us (level)
  no operation moved by 1% of the time
where the time goes in v5:
time: 27 us; the launch traced here: 26.9 us
  Pallas kernels  26.2 us (97%)
  local copies, waits for them, and re-layouts  0.66 us (2%)
    pallas_call x1, Pallas kernels, body(): pl.pallas_call(functools.partial(kernel, n_mem, n_lon), out_shape=pltpu.V...  26.2 us
    unnamed x1, local copies, waits for them, and re-layouts  0.66 us

profile of v5, /device:TPU:2, one launch (start us, length us, event | category | flops | bytes accessed | tf_op | source)
XLA Modules:
  0.0 26.9 jit_solution(14843675009938109198)
XLA Ops:
  0.0 26.2 %shard_map.64 = bf16[16,4096]{1,0:T(8,128)(2,1)S(1)} custom-call(bf16[16,4096]{1,0:T(8,128)(2,1)} %state_ref.1, bf16[32,256,128]{2,1,0:T(8,128)(2,1)} %hx_ref.1, f32[32,128]{1,0:T(8,128)} %value_hbm.1, f32[32,128]{1,0:T(8,128)} %rinv_hbm.1, s32[32]{0:T(128)} %count_hbm.1, s32[8,32]{1,0:T(8,128)} %bitcast.1), custom_call_target="tpu_custom_call" | custom-call | tf_op jit(solution)/shard_map/pallas_call | solution.py:327
  26.2 0.7 %copy.8 = bf16[16,4096]{1,0:T(8,128)(2,1)} copy(bf16[16,4096]{1,0:T(8,128)(2,1)S(1)} %shard_map.64) | data formatting | bytes 262144

commit v6 on v5

--- a/solution.py
+++ b/solution.py
@@ -72,8 +72,6 @@
         order.append(column * 2 + 1 - x)
         if step:
             order.append(column * 2 + x)
-    for peer in order:
-        signal(barrier, peer, lon)
 
     smalls = []
     for i, (src, dst) in enumerate(
@@ -93,6 +91,8 @@
     mine_cols = pl.ds(pl.multiple_of(mem * cols, cols), cols)
     keep = pltpu.make_async_copy(state_ref.at[:, mine_cols], gathered.at[mine_rows, :], here_sem.at[0])
     keep.start()
+    for peer in order:
+        signal(barrier, peer, lon)
     for move in smalls:
         move.wait()
 

time: 27 us -> 27 us (level)
  no operation moved by 1% of the time
where the time goes in v6:
time: 27 us; the launch traced here: 26.9 us
  Pallas kernels  26.2 us (97%)
  local copies, waits for them, and re-layouts  0.66 us (2%)
    pallas_call x1, Pallas kernels, body(): pl.pallas_call(functools.partial(kernel, n_mem, n_lon), out_shape=pltpu.V...  26.2 us
    unnamed x1, local copies, waits for them, and re-layouts  0.66 us

profile of v6, /device:TPU:2, one launch (start us, length us, event | category | flops | bytes accessed | tf_op | source)
XLA Modules:
  0.0 26.9 jit_solution(9996243178595074583)
XLA Ops:
  0.0 26.2 %shard_map.64 = bf16[16,4096]{1,0:T(8,128)(2,1)S(1)} custom-call(bf16[16,4096]{1,0:T(8,128)(2,1)} %state_ref.1, bf16[32,256,128]{2,1,0:T(8,128)(2,1)} %hx_ref.1, f32[32,128]{1,0:T(8,128)} %value_hbm.1, f32[32,128]{1,0:T(8,128)} %rinv_hbm.1, s32[32]{0:T(128)} %count_hbm.1, s32[8,32]{1,0:T(8,128)} %bitcast.1), custom_call_target="tpu_custom_call" | custom-call | tf_op jit(solution)/shard_map/pallas_call | solution.py:327
  26.2 0.7 %copy.8 = bf16[16,4096]{1,0:T(8,128)(2,1)} copy(bf16[16,4096]{1,0:T(8,128)(2,1)S(1)} %shard_map.64) | data formatting | bytes 262144
